TPU v7x, 32 devices: a whole 2x2x4 slice. The times are simulated.
32 devices in a mesh: rows: 8 (over y, x, core), cols: 4 (over z).
Axes of the slice: x: 2, y: 2, z: 4, core: 2. Of those that a mesh axis runs over, the one named last changes fastest.
Arguments:
- block_values: bfloat16 [16384, 128], P(('rows', 'cols')), may hold values from -6 to 6
- block_length: int32 [16384], P(('rows', 'cols')), may hold values from 1 to 128
- block_owner: int32 [16384], P(('rows', 'cols')), may hold values from 0 to 4095, as said below
- block_second: int32 [16384], P(('rows', 'cols')), may hold values from 0 to 4095, as said below
- block_third: int32 [16384, 128], P(('rows', 'cols')), may hold values from 0 to 8191
- live_blocks: int32 [32], P(('rows', 'cols')), may hold values from 1 to 512, as said below
- second_factor: bfloat16 [4096, 256], P('cols', 'rows')
- third_factor: bfloat16 [8192, 256], P('cols', 'rows'), may hold values from -6 to 6
Outputs:
- first_factor: float32 [4096, 256], P('cols', 'rows')
Inputs may be any that keep to these rules, and one draw needn't show every extreme that they name: `block_owner`: slot b lies on device d = b // 512 with index r along rows; its row lies in r * 4096 // 8 up to (r + 1) * 4096 // 8 - 1, the device's mode-1 slab. `block_second`: slot b lies on device d = b // 512 with index c along cols; its row lies in c * 4096 // 4 up to (c + 1) * 4096 // 4 - 1. `live_blocks`: some device uses all 512 slots in every draw.
All inputs are finite; a program needn't handle non-finite values.
Results may differ from a plain program's by a relative error of at most 0.0003.
Values may be sent and summed in bfloat16 or wider, within the bound.
A program may use at most 128 MiB of HBM per device.

v0:
```python
import jax
import jax.numpy as jnp
from jax import lax
from jax.sharding import PartitionSpec as P

I_DEV = 128


def gram_product(left, right):
    contract = (((0,), (0,)), ((), ()))
    return lax.dot_general(left, right, contract, preferred_element_type=jnp.float32)


def block_fold(values, third, table):
    group = values.shape[0]
    width = values.shape[1]
    picked = table[third.reshape(group * width)]
    scaled = values.reshape(group * width, 1).astype(jnp.float32) * picked.astype(jnp.float32)
    return jnp.sum(scaled.reshape(group, width, picked.shape[1]), axis=1)


def per_device(
    block_values,
    block_length,
    block_owner,
    block_second,
    block_third,
    live_blocks,
    second_factor,
    third_factor,
):
    n_rows = lax.axis_size("rows")
    n_cols = lax.axis_size("cols")
    row_at = lax.axis_index("rows")
    col_at = lax.axis_index("cols")
    contract = (((0,), (0,)), ((), ()))
    width = block_values.shape[1]
    lane = jnp.arange(width, dtype=jnp.int32)
    slab = I_DEV * n_cols
    owned = jnp.arange(slab, dtype=jnp.int32)
    second_range = lax.all_gather(second_factor, "rows", axis=1, tiled=True)
    third_part = lax.all_gather(third_factor, "cols", axis=0, tiled=True)
    third_whole = lax.all_gather(third_part, "rows", axis=1, tiled=True)
    range_rows = second_range.shape[0]
    local_gram = gram_product(second_range, second_range)
    gram_second = lax.psum(local_gram, "cols") / (range_rows * n_cols)
    gram_third = gram_product(third_whole, third_whole) / third_whole.shape[0]
    gram = gram_second * gram_third
    nblk = block_values.shape[0]
    group = min(nblk, 128)
    count = live_blocks[0]

    def accumulate(step, total):
        start = step * group
        values = lax.dynamic_slice_in_dim(block_values, start, group, 0)
        lengths = lax.dynamic_slice_in_dim(block_length, start, group, 0)
        third = lax.dynamic_slice_in_dim(block_third, start, group, 0)
        second = lax.dynamic_slice_in_dim(block_second, start, group, 0)
        owner = lax.dynamic_slice_in_dim(block_owner, start, group, 0)
        slot = start + jnp.arange(group, dtype=jnp.int32)
        live = (lane[None, :] < lengths[:, None]) & (slot < count)[:, None]
        values = jnp.where(live, values, jnp.zeros((), jnp.bfloat16))
        fold = block_fold(values, third, third_whole)
        contrib = second_range[second - col_at * range_rows].astype(jnp.float32) * fold
        onehot = ((owner - row_at * slab)[:, None] == owned[None, :]).astype(jnp.float32)
        return total + lax.dot_general(
            onehot,
            contrib,
            contract,
            precision=lax.Precision.HIGHEST,
            preferred_element_type=jnp.float32,
        )

    start_total = jnp.zeros((slab, gram.shape[0]), jnp.float32)
    partial_rows = lax.fori_loop(0, (count + group - 1) // group, accumulate, start_total)
    mine = lax.psum_scatter(partial_rows, "cols", scatter_dimension=0, tiled=True)
    factor = jnp.linalg.cholesky(gram)
    solved = jax.scipy.linalg.cho_solve((factor, True), mine.T).T
    moved = lax.all_to_all(
        lax.all_to_all(solved, "rows", split_axis=1, concat_axis=0, tiled=True),
        "cols",
        split_axis=0,
        concat_axis=0,
        tiled=True,
    )
    share = n_rows // n_cols
    owned_rows = mine.shape[0]
    reordered = moved.reshape(n_cols, share, owned_rows, moved.shape[1]).transpose(1, 0, 2, 3)
    return reordered.reshape(n_rows * owned_rows, moved.shape[1])


def solution(mesh):
    return jax.shard_map(
        per_device,
        mesh=mesh,
        in_specs=(
            P(("rows", "cols"), None),
            P(("rows", "cols")),
            P(("rows", "cols")),
            P(("rows", "cols")),
            P(("rows", "cols"), None),
            P(("rows", "cols")),
            P("cols", "rows"),
            P("cols", "rows"),
        ),
        out_specs=P("cols", "rows"),
        check_vma=False,
    )
```

profile of v0, /device:TPU:0, one launch (start us, length us, event | category | flops | bytes accessed | tf_op | source)
XLA Modules:
  0.0 476.4 jit_solution(10479192141841204088)
XLA Ops:
  7.4 11.6 %all_gather.9 = bf16[1024,256]{0,1:T(8,128)(2,1)S(1)} all-gather(bf16[1024,32]{0,1:T(8,128)(2,1)} %param.16), channel_id=1, replica_groups=mesh['rows'=8,'cols'=4] {'rows'}, dimensions={1}, use_global_device_ids=true | all-gather | bytes 589824 | tf_op jit(solution)/shard_map/all_gather | solution.py:41
  19.0 1.1 fusion.24
  20.1 20.9 %all_gather.10 = bf16[8192,32]{0,1:T(8,128)(2,1)} all-gather(bf16[2048,32]{0,1:T(8,128)(2,1)} %param.17), channel_id=1, replica_groups=mesh['rows'=8,'cols'=4] {'cols'}, dimensions={0}, use_global_device_ids=true | all-gather | bytes 655360 | tf_op jit(solution)/shard_map/all_gather | solution.py:42
  42.0 15.7 %all-reduce.3.cloned.1.call-done = f32[256,256]{0,1:T(8,128)} async-done(((f32[256,256]{0,1:T(8,128)}), f32[256,256]{0,1:T(8,128)}) %all-reduce.3.cloned.1.call-update) | async-done | bytes 262160 | tf_op jit(solution)/shard_map/psum | solution.py:46
  57.7 18.4 %all-gather.2.cloned.1.call-done = bf16[8192,256]{0,1:T(8,128)(2,1)} async-done(((bf16[8192,32]{0,1:T(8,128)(2,1)}), bf16[8192,256]{0,1:T(8,128)(2,1)}) %all-gather.2.cloned.1.call-update) | async-done | bytes 4194320 | tf_op jit(solution)/shard_map/all_gather | solution.py:43
  76.1 4.7 fusion.11
  81.1 11.7 %cholesky.50 = f32[128,128]{1,0:T(8,128)S(1)} custom-call(f32[128,128]{1,0:T(8,128)S(1)} %cholesky.118), custom_call_target="Cholesky" | custom-call | tf_op jit(solution)/shard_map/jit(cholesky)/cholesky | solution.py:77
  92.8 9.8 %custom-call.18 = f32[1,128,128]{1,2,0:T(8,128)S(1)} custom-call(f32[1,128,128]{2,1,0:T(8,128)S(1)} %get-tuple-element.274), custom_call_target="InvertDiagBlocksLowerTriangular" | custom-call | tf_op jit(solution)/shard_map/jit(cholesky)/cholesky | solution.py:77
  103.1 11.7 %cholesky.105 = f32[128,128]{1,0:T(8,128)S(1)} custom-call(f32[128,128]{1,0:T(8,128)S(1)} %convolution_subtract_fusion.2), custom_call_target="Cholesky" | custom-call | tf_op jit(solution)/shard_map/jit(cholesky)/cholesky | solution.py:77
  114.8 6.4 %copy.34 = bf16[8192,256]{1,0:T(8,128)(2,1)} copy(bf16[8192,256]{0,1:T(8,128)(2,1)} %all-gather.2.cloned.1.call-done) | data formatting | bytes 8388608
  121.3 149.3 %while.15 = (s32[]{:T(128)}, f32[512,256]{1,0:T(8,128)S(1)}, s32[]{:T(128)}, s32[512]{0:T(512)}, s32[]{:T(128)}, /*index=5*/s32[512]{0:T(512)}, s32[]{:T(128)}, ...) while((s32[]{:T(128)}, f32[512,256]{1,0:T(8,128)S(1)}, ...), condition=%wide.region_7.8_spmd.clone, body=%wide.region_5.7_spmd.clone.sunk | while | flops 214271872 | bytes 27305452 | solution.py:75
  124.7 63.5 %gather_fusion = bf16[16384,256]{1,0:T(8,128)(2,1)} fusion(bf16[8192,256]{1,0:T(8,128)(2,1)} %get-tuple-element.438, s32[16384]{0:T(1024)S(1)} %broadcast_clamp_fusion.2), kind=kCustom, calls=%fused_computation.1.clone.clone.1 | custom fusion | bytes 16842752 | tf_op jit(solution)/shard_map/while/body/gather | solution.py:17
  188.2 5.5 %fusion.43 = f32[128,256]{1,0:T(8,128)S(1)} fusion(f32[128,128]{1,0:T(8,128)S(1)} %fusion.42, bf16[16384,256]{1,0:T(8,128)(2,1)} %gather_fusion), kind=kLoop, calls=%fused_computation.7.clone.1 | loop fusion | flops 12550144 | bytes 8585216 | tf_op jit(solution)/shard_map/while/body/reduce_sum | solution.py:19
  199.2 63.5 %gather_fusion = bf16[16384,256]{1,0:T(8,128)(2,1)} fusion(bf16[8192,256]{1,0:T(8,128)(2,1)} %get-tuple-element.438, s32[16384]{0:T(1024)S(1)} %broadcast_clamp_fusion.2), kind=kCustom, calls=%fused_computation.1.clone.clone.1 | custom fusion | bytes 16842752 | tf_op jit(solution)/shard_map/while/body/gather | solution.py:17
  262.8 5.5 %fusion.43 = f32[128,256]{1,0:T(8,128)S(1)} fusion(f32[128,128]{1,0:T(8,128)S(1)} %fusion.42, bf16[16384,256]{1,0:T(8,128)(2,1)} %gather_fusion), kind=kLoop, calls=%fused_computation.7.clone.1 | loop fusion | flops 12550144 | bytes 8585216 | tf_op jit(solution)/shard_map/while/body/reduce_sum | solution.py:19
  273.6 3.9 while.14
  274.2 1.3 bitcast_dynamic-update-slice_fusion.2
  276.2 1.3 bitcast_dynamic-update-slice_fusion.2
  277.5 19.7 %custom-call.19 = f32[2,128,128]{1,2,0:T(8,128)S(1)} custom-call(f32[2,128,128]{2,1,0:T(8,128)S(1)} %get-tuple-element.189), custom_call_target="InvertDiagBlocksLowerTriangular" | custom-call | tf_op jit(solution)/shard_map/jit(_cho_solve)/triangular_solve | solution.py:78
  297.2 145.4 %reduce-scatter.2.cloned.1.call-done = f32[128,256]{0,1:T(8,128)} async-done(((f32[512,256]{0,1:T(8,128)}), f32[128,256]{0,1:T(8,128)}) %reduce-scatter.2.cloned.1.call-update) | async-done | bytes 131088 | tf_op jit(solution)/shard_map/reduce_scatter | solution.py:76
  442.6 1.1 fusion.13
  443.7 1.0 convolution_subtract_fusion.1
  445.8 11.4 %all_to_all.25 = f32[128,8,32]{0,2,1:T(8,128)S(1)} all-to-all(f32[128,8,32]{0,2,1:T(8,128)S(1)} %bitcast.67), channel_id=1, replica_groups=mesh['rows'=8,'cols'=4] {'rows'}, dimensions={1} | all-to-all | bytes 262144 | tf_op jit(solution)/shard_map/all_to_all | solution.py:80
  457.4 10.7 %all_to_all.26 = f32[4,256,32]{1,2,0:T(8,128)S(1)} all-to-all(f32[4,256,32]{1,2,0:T(8,128)S(1)} %copy.37), channel_id=1, replica_groups=mesh['rows'=8,'cols'=4] {'cols'}, dimensions={0} | all-to-all | bytes 262144 | tf_op jit(solution)/shard_map/all_to_all | solution.py:79
  (57 shorter events, 17.1 us)
Async XLA Ops:
  7.4 50.3 %all-reduce.3.cloned.1.call-start = ((), (), s32[]{:S(2)}) async-start(), calls=%async_computation.3 | async-start | bytes 524288 | tf_op jit(solution)/shard_map/psum | solution.py:46
  20.1 56.0 %all-gather.2.cloned.1.call-start = ((), (), s32[]{:S(2)}) async-start(), calls=%async_computation.4 | async-start | bytes 4718592 | tf_op jit(solution)/shard_map/all_gather | solution.py:43
  41.0 401.6 %reduce-scatter.2.cloned.1.call-start = ((), (), s32[]{:S(2)}) async-start(), calls=%async_computation.5 | async-start | bytes 655360 | tf_op jit(solution)/shard_map/reduce_scatter | solution.py:76
Sparse Core Ops, SparseCore 0:
  20.2 37.4 all-reduce.2
  271.7 170.9 reduce-scatter.1
Sparse Core Ops, SparseCore 1:
  41.1 34.9 all-gather.1
where the time goes:
time: 478 us; the launch traced here: 476 us
  waiting for transfers between devices  180 us (38%)
  local copies, waits for them, and re-layouts  145 us (30%)
  other arithmetic  69.4 us (15%)
  blocking collectives  54.6 us (11%)
  between operations  17 us (4%)
  matrix products  10.7 us (2%)
    reduce_scatter x1, waiting for transfers between devices, per_device(): lax.psum_scatter(partial_rows, 'cols', scatter_dimension=0, tiled=True)  145 us
    gather x2, local copies, waits for them, and re-layouts, block_fold(): picked = table[third.reshape(group * width)]  127 us
    another operation x6, other arithmetic, per_device(): factor = jnp.linalg.cholesky(gram)  34 us
    all_gather x1, blocking collectives, per_device(): third_part = lax.all_gather(third_factor, 'cols', axis=0, tiled=True)  20.9 us
    another operation x4, other arithmetic, per_device(): solved = jax.scipy.linalg.cho_solve((factor, True), mine.T).T  19.7 us
    all_gather x1, waiting for transfers between devices, per_device(): third_whole = lax.all_gather(third_part, 'rows', axis=1, tiled=True)  18.4 us
    psum x1, waiting for transfers between devices, per_device(): gram_second = lax.psum(local_gram, 'cols') / (range_rows * n_cols)  15.7 us
    all_gather x1, blocking collectives, per_device(): second_range = lax.all_gather(second_factor, 'rows', axis=1, tiled=True)  11.6 us
  transfers between devices with their start and end apart: 3, of which 3 were waited for; matrix products, arithmetic and copies ran while one was open for 5% of the time, Pallas kernels for 0%

commit v1 on v0

v1 whole, which is shorter than its diff:
```python
import functools

import jax
import jax.numpy as jnp
from jax import lax
from jax.experimental import pallas as pl
from jax.experimental.pallas import tpu as pltpu
from jax.sharding import PartitionSpec as P

LO = 256
BF = jnp.bfloat16
F32 = jnp.float32
NT = (((1,), (1,)), ((), ()))
NN = (((1,), (0,)), ((), ()))
TN = (((0,), (0,)), ((), ()))


def dot(a, b, dims, precision=None):
    return lax.dot_general(a, b, dims, precision=precision, preferred_element_type=F32)


def spread_kernel(group, n_hi, count_ref, values_ref, length_ref, third_ref, high_ref, low_ref, masked, rows):
    width = values_ref.shape[1]
    base = pl.program_id(0) * group
    lane = lax.broadcasted_iota(jnp.int32, (group, width), 1)
    slot = lax.broadcasted_iota(jnp.int32, (group, width), 0) + base
    live = (lane < length_ref[...]) & (slot < count_ref[0])
    masked[...] = jnp.where(live, values_ref[...].astype(F32), 0.0)
    at_hi = lax.broadcasted_iota(jnp.int32, (n_hi, width), 0)
    at_lo = lax.broadcasted_iota(jnp.int32, (LO, width), 0)

    def eight(step, carry):
        first = pl.multiple_of(step * 8, 8)
        index = third_ref[pl.ds(first, 8), :]
        value = masked[pl.ds(first, 8), :]
        index_hi = index // LO
        index_lo = index - index_hi * LO
        for j in range(8):
            left = jnp.where(at_hi == index_hi[j : j + 1, :], value[j : j + 1, :], 0.0).astype(BF)
            right = jnp.where(at_lo == index_lo[j : j + 1, :], 1.0, 0.0).astype(BF)
            dense = dot(left, right, NT)
            start = pl.multiple_of((first + j) * n_hi, n_hi)
            for piece in range(LO // 128):
                rows[piece, pl.ds(start, n_hi), :] = dense[:, piece * 128 : (piece + 1) * 128]
        return carry

    lax.fori_loop(0, group // 8, eight, 0)
    for h in range(n_hi):
        for piece in range(LO // 128):
            part = rows[piece, pl.ds(h, group, stride=n_hi), :]
            high = part.astype(BF)
            high_ref[h, :, piece * 128 : (piece + 1) * 128] = high
            low_ref[h, :, piece * 128 : (piece + 1) * 128] = (part - high.astype(F32)).astype(BF)


def spread(count, values, length, third, n_hi):
    nblk, width = values.shape
    group = min(nblk, 64)
    return pl.pallas_call(
        functools.partial(spread_kernel, group, n_hi),
        grid=(nblk // group,),
        in_specs=[
            pl.BlockSpec(memory_space=pltpu.SMEM),
            pl.BlockSpec((group, width), lambda g: (g, 0)),
            pl.BlockSpec((group, 1), lambda g: (g, 0)),
            pl.BlockSpec((group, width), lambda g: (g, 0)),
        ],
        out_specs=[pl.BlockSpec((n_hi, group, LO), lambda g: (0, g, 0))] * 2,
        out_shape=[jax.ShapeDtypeStruct((n_hi, nblk, LO), BF)] * 2,
        scratch_shapes=[pltpu.VMEM((group, width), F32), pltpu.VMEM((LO // 128, group * n_hi, 128), F32)],
        compiler_params=pltpu.CompilerParams(vmem_limit_bytes=40 * 1024 * 1024),
        cost_estimate=pl.CostEstimate(flops=20_000_000_000, bytes_accessed=4 * n_hi * nblk * LO, transcendentals=0),
        name="spread",
    )(count, values, length, third)


def fold_kernel(per, high_ref, low_ref, third_ref, second_ref, pick_ref, owner_ref, out_ref, fold):
    step = pl.program_id(0)
    nblk = fold.shape[0]

    @pl.when(step == 0)
    def _():
        fold[...] = jnp.zeros_like(fold)

    total = None
    for h in range(per):
        table = third_ref[h * LO : (h + 1) * LO, :]
        term = dot(high_ref[h], table, NN) + dot(low_ref[h], table, NN)
        total = term if total is None else total + term
    fold[...] += total

    @pl.when(step == pl.num_programs(0) - 1)
    def _():
        at = lax.broadcasted_iota(jnp.int32, (nblk, second_ref.shape[0]), 1)
        pick = jnp.where(at == pick_ref[...], 1.0, 0.0).astype(BF)
        contrib = dot(pick, second_ref[...], NN) * fold[...]
        at = lax.broadcasted_iota(jnp.int32, (out_ref.shape[0], nblk), 0)
        place = jnp.where(at == owner_ref[...], 1.0, 0.0).astype(BF)
        high = contrib.astype(BF)
        rest = contrib - high.astype(F32)
        middle = rest.astype(BF)
        low = (rest - middle.astype(F32)).astype(BF)
        out_ref[...] = dot(place, high, NN) + (dot(place, middle, NN) + dot(place, low, NN))


def fold_rows(high, low, third, second, pick, owner, slab):
    n_hi, nblk, lo = high.shape
    rank = third.shape[1]
    per = min(n_hi, 4)
    return pl.pallas_call(
        functools.partial(fold_kernel, per),
        grid=(n_hi // per,),
        in_specs=[
            pl.BlockSpec((per, nblk, lo), lambda g: (g, 0, 0)),
            pl.BlockSpec((per, nblk, lo), lambda g: (g, 0, 0)),
            pl.BlockSpec((per * lo, rank), lambda g: (g, 0)),
            pl.BlockSpec(second.shape, lambda g: (0, 0)),
            pl.BlockSpec((nblk, 1), lambda g: (0, 0)),
            pl.BlockSpec((1, nblk), lambda g: (0, 0)),
        ],
        out_specs=pl.BlockSpec((slab, rank), lambda g: (0, 0)),
        out_shape=jax.ShapeDtypeStruct((slab, rank), F32),
        scratch_shapes=[pltpu.VMEM((nblk, rank), F32)],
        compiler_params=pltpu.CompilerParams(vmem_limit_bytes=50 * 1024 * 1024),
        cost_estimate=pl.CostEstimate(flops=10_000_000_000, bytes_accessed=4 * n_hi * nblk * lo, transcendentals=0),
        name="fold_rows",
    )(high, low, third, second, pick, owner)


def small_inverse(block):
    n = block.shape[0]
    down = lax.broadcasted_iota(jnp.int32, (n, n), 0)
    across = lax.broadcasted_iota(jnp.int32, (n, n), 1)
    for j in range(n):
        column = block[:, j : j + 1]
        pivot = 1.0 / block[j : j + 1, j : j + 1]
        cleared = jnp.where(across == j, jnp.where(down == j, 1.0, 0.0), block)
        row = cleared[j : j + 1, :] * pivot
        block = jnp.where(down == j, row, cleared - column * row)
    return block


def invert_kernel(size, gram_ref, out_ref):
    rank = gram_ref.shape[1]
    exact = lax.Precision.HIGHEST
    a = gram_ref[0] * gram_ref[1]
    down = lax.broadcasted_iota(jnp.int32, (rank, size), 0)
    eye = jnp.where(
        lax.broadcasted_iota(jnp.int32, (size, size), 0) == lax.broadcasted_iota(jnp.int32, (size, size), 1), 1.0, 0.0
    )
    for k in range(rank // size):
        s, e = k * size, (k + 1) * size
        inverse = small_inverse(a[s:e, s:e])
        column = jnp.where((down >= s) & (down < e), 0.0, a[:, s:e])
        pieces = [a[s:e, :s]] * (s > 0) + [eye] + [a[s:e, e:]] * (e < rank)
        row = dot(inverse, jnp.concatenate(pieces, axis=1), NN, exact)
        zero = jnp.zeros((rank, size), F32)
        pieces = [a[:, :s]] * (s > 0) + [zero] + [a[:, e:]] * (e < rank)
        a = jnp.concatenate(pieces, axis=1) - dot(column, row, NN, exact)
        pieces = [a[:s]] * (s > 0) + [row] + [a[e:]] * (e < rank)
        a = jnp.concatenate(pieces, axis=0)
    out_ref[...] = a


def invert(grams):
    rank = grams.shape[1]
    return pl.pallas_call(
        functools.partial(invert_kernel, 32),
        out_shape=jax.ShapeDtypeStruct((rank, rank), F32),
        cost_estimate=pl.CostEstimate(flops=10_000_000_000, bytes_accessed=1_000_000, transcendentals=0),
        name="invert",
    )(grams)


def per_device(
    block_values,
    block_length,
    block_owner,
    block_second,
    block_third,
    live_blocks,
    second_factor,
    third_factor,
):
    n_rows = lax.axis_size("rows")
    n_cols = lax.axis_size("cols")
    row_at = lax.axis_index("rows")
    col_at = lax.axis_index("cols")
    nblk = block_values.shape[0]
    range_rows = second_factor.shape[0]
    third_rows = third_factor.shape[0]
    whole_third = third_rows * n_cols
    slab = range_rows * n_cols // n_rows

    both = lax.all_gather(jnp.concatenate([third_factor, second_factor], axis=0), "rows", axis=1, tiled=True)
    third_range = both[:third_rows]
    second_range = both[third_rows:]
    third_whole = lax.all_gather(third_range, "cols", axis=0, tiled=True)
    grams = jnp.stack(
        [
            dot(second_range, second_range, TN) / (range_rows * n_cols),
            dot(third_range, third_range, TN) / whole_third,
        ]
    )
    inverse = invert(lax.psum(grams, "cols"))

    high, low = spread(live_blocks, block_values, block_length[:, None], block_third, whole_third // LO)
    partial_rows = fold_rows(
        high,
        low,
        third_whole,
        second_range,
        (block_second - col_at * range_rows)[:, None],
        (block_owner - row_at * slab)[None, :],
        slab,
    )
    mine = lax.psum_scatter(partial_rows, "cols", scatter_dimension=0, tiled=True)
    solved = dot(mine, inverse, NN, lax.Precision.HIGHEST)
    moved = lax.all_to_all(
        lax.all_to_all(solved, "rows", split_axis=1, concat_axis=0, tiled=True),
        "cols",
        split_axis=0,
        concat_axis=0,
        tiled=True,
    )
    share = n_rows // n_cols
    owned_rows = mine.shape[0]
    reordered = moved.reshape(n_cols, share, owned_rows, moved.shape[1]).transpose(1, 0, 2, 3)
    return reordered.reshape(n_rows * owned_rows, moved.shape[1])


def solution(mesh):
    return jax.shard_map(
        per_device,
        mesh=mesh,
        in_specs=(
            P(("rows", "cols"), None),
            P(("rows", "cols")),
            P(("rows", "cols")),
            P(("rows", "cols")),
            P(("rows", "cols"), None),
            P(("rows", "cols")),
            P("cols", "rows"),
            P("cols", "rows"),
        ),
        out_specs=P("cols", "rows"),
        check_vma=False,
    )
```

time: 478 us -> 217 us (0.45)
  local copies, waits for them, and re-layouts: 145 us -> 8.53 us
  waiting for transfers between devices: 180 us -> 93.3 us
  Pallas kernels: 0 us -> 77 us
  other arithmetic: 69.4 us -> 2.52 us
  blocking collectives: 54.6 us -> 18.2 us
  matrix products: 10.7 us -> 2.41 us
    reduce_scatter x1, waiting for transfers between devices: 145 us -> 0.01 us  [per_device(): lax.psum_scatter(partial_rows, 'cols', scatter_dimension=0, tiled=True)]
    gather x4 -> x0, local copies, waits for them, and re-layouts: 129 us -> none  [the longest x2 127 us: block_fold(): picked = table[third.reshape(group * width)]]
    pallas_call x0 -> x3, Pallas kernels: none -> 77 us  [the longest x1 35.5 us: spread(): pl.pallas_call(functools.partial(spread_kernel, group, n_hi), grid=(nblk...]
    another operation x10 -> x1, other arithmetic: 53.7 us -> 0.87 us  [per_device(): jnp.stack([dot(second_range, second_range, TN) / (range_rows * n_cols), d...]
    all_gather x1 -> x2, waiting for transfers between devices: 18.4 us -> 67.1 us  [the longest x1 37.8 us: per_device(): third_whole = lax.all_gather(third_range, 'cols', axis=0, tiled=True)]
    all_gather x2 -> x0, blocking collectives: 32.5 us -> none  [the longest x1 20.9 us: per_device(): third_part = lax.all_gather(third_factor, 'cols', axis=0, tiled=True)]
    reduce_sum x2 -> x0, other arithmetic: 10.9 us -> none  [block_fold(): return jnp.sum(scaled.reshape(group, width, picked.shape[1]), axis=1)]
    psum x1, waiting for transfers between devices: 15.7 us -> 26.2 us  [per_device(): inverse = invert(lax.psum(grams, 'cols'))]
  transfers between devices with their start and end apart: 3 -> 4, of which waited for: 3 -> 3; matrix products, arithmetic and copies ran while one was open for 5% -> 1% of each run, Pallas kernels for 0% -> 36%
where the time goes in v1:
time: 217 us; the launch traced here: 216 us
  waiting for transfers between devices  93.3 us (43%)
  Pallas kernels  77 us (35%)
  blocking collectives  18.2 us (8%)
  between operations  13.9 us (6%)
  local copies, waits for them, and re-layouts  8.53 us (4%)
  other arithmetic  2.52 us (1%)
  matrix products  2.41 us (1%)
    all_gather x1, waiting for transfers between devices, per_device(): third_whole = lax.all_gather(third_range, 'cols', axis=0, tiled=True)  37.8 us
    pallas_call x1, Pallas kernels, spread(): pl.pallas_call(functools.partial(spread_kernel, group, n_hi), grid=(nblk...  35.5 us
    all_gather x1, waiting for transfers between devices, per_device(): lax.all_gather(jnp.concatenate([third_factor, second_factor], axis=0), 'r...  29.3 us
    pallas_call x1, Pallas kernels, invert(): pl.pallas_call(functools.partial(invert_kernel, 32), out_shape=jax.ShapeD...  28.2 us
    psum x1, waiting for transfers between devices, per_device(): inverse = invert(lax.psum(grams, 'cols'))  26.2 us
    pallas_call x1, Pallas kernels, fold_rows(): pl.pallas_call(functools.partial(fold_kernel, per), grid=(n_hi // per,),...  13.3 us
    all_to_all x1, blocking collectives, per_device(): lax.all_to_all(lax.all_to_all(solved, 'rows', split_axis=1, concat_axis=0...  9.27 us
    all_to_all x1, blocking collectives, per_device(): lax.all_to_all(solved, 'rows', split_axis=1, concat_axis=0, tiled=True)  8.95 us
  transfers between devices with their start and end apart: 4, of which 3 were waited for; matrix products, arithmetic and copies ran while one was open for 1% of the time, Pallas kernels for 36%

profile of v1, /device:TPU:0, one launch (start us, length us, event | category | flops | bytes accessed | tf_op | source)
XLA Modules:
  0.0 216.2 jit_solution(5033507533155792213)
XLA Ops:
  6.5 1.6 pad_maximum_fusion.1
  8.3 29.3 %all-gather.3.cloned.1.call-done = bf16[3072,256]{0,1:T(8,128)(2,1)} async-done(((bf16[3072,32]{0,1:T(8,128)(2,1)}), bf16[3072,256]{0,1:T(8,128)(2,1)}) %all-gather.3.cloned.1.call-update) | async-done | bytes 1572880 | tf_op jit(solution)/shard_map/all_gather | solution.py:195
  37.5 1.2 slice-done
  38.8 1.3 copy.35
  40.8 0.1 copy.29.pick_ref
  41.0 0.1 copy.26.length_ref
  41.2 35.5 %spread.1 = (bf16[32,512,256]{2,1,0:T(8,128)(2,1)S(1)}, bf16[32,512,256]{2,1,0:T(8,128)(2,1)}) custom-call(s32[1]{0:T(128)S(6)} %copy.38.count_ref, bf16[512,128]{1,0:T(8,128)(2,1)S(1)} %copy-done.1, s32[512,1]{1,0:T(8,128)S(1)} %copy.26.length_ref, s32[512,128]{1,0:T(8,128)S(1)} %copy-done), custom_call_target="tpu_custom_call" | custom-call | flops 20000000000 | bytes 16777216 | tf_op jit(solution)/shard_map/spread/pallas_call | solution.py:59
  76.7 3.2 %copy-done.2 = bf16[32,512,256]{2,1,0:T(8,128)(2,1)} copy-done((bf16[32,512,256]{2,1,0:T(8,128)(2,1)}, bf16[32,512,256]{2,1,0:T(8,128)(2,1)S(1)}, u32[]{:S(2)}) %copy-start.2) | copy-done | bytes 8388632
  79.9 0.2 copy.36.second_ref
  80.1 1.2 copy-done.3
  81.3 0.3 fusion
  81.7 0.5 fusion.1
  82.2 0.9 pad_maximum_fusion
  83.0 0.2 reduce-scatter.2.cloned.1.call-start
  83.3 37.8 %all-gather.5.cloned.1.call-done.third_ref = bf16[8192,256]{1,0:T(8,128)(2,1)} async-done(((bf16[2048,256]{1,0:T(8,128)(2,1)}), bf16[8192,256]{1,0:T(8,128)(2,1)}) %all-gather.5.cloned.1.call-update) | async-done | bytes 4194320 | tf_op jit(solution)/shard_map/all_gather | solution.py:198
  121.1 13.3 %fold_rows.1 = f32[512,256]{1,0:T(8,128)} custom-call(bf16[32,512,256]{2,1,0:T(8,128)(2,1)} %copy-done.2, bf16[32,512,256]{2,1,0:T(8,128)(2,1)} %get-tuple-element.8.low_ref, bf16[8192,256]{1,0:T(8,128)(2,1)} %all-gather.5.cloned.1.call-done.third_ref, bf16[1024,256]{1,0:T(8,128)(2,1)S(1)} %copy.36.second_ref, s32[512,1]{1,0:T(8,128)S(1)} %copy.29.pick_ref, ...), custom_call_target="tpu_custom_call" | custom-call | flops 10000000000 | bytes 16777216 | tf_op jit(solution)/shard_map/fold_rows/pallas_call | solution.py:110
  134.4 26.2 %all-reduce.2.cloned.1.call-done.gram_ref = f32[2,256,256]{2,1,0:T(8,128)} async-done(((f32[2,256,256]{2,1,0:T(8,128)}), f32[2,256,256]{2,1,0:T(8,128)}) %all-reduce.2.cloned.1.call-update) | async-done | bytes 524304 | tf_op jit(solution)/shard_map/psum | solution.py:205
  160.6 28.2 %invert.1 = f32[256,256]{1,0:T(8,128)} custom-call(f32[2,256,256]{2,1,0:T(8,128)} %all-reduce.2.cloned.1.call-done.gram_ref), custom_call_target="tpu_custom_call" | custom-call | flops 10000000000 | bytes 1000000 | tf_op jit(solution)/shard_map/invert/pallas_call | solution.py:167
  188.8 1.6 fusion.4
  190.4 8.9 %all_to_all.25 = f32[128,8,32]{0,2,1:T(8,128)S(1)} all-to-all(f32[128,8,32]{0,2,1:T(8,128)S(1)} %bitcast.21), channel_id=1, replica_groups=mesh['rows'=8,'cols'=4] {'rows'}, dimensions={1} | all-to-all | bytes 262144 | tf_op jit(solution)/shard_map/all_to_all | solution.py:220
  199.4 0.1 copy.31
  199.6 9.3 %all_to_all.26 = f32[4,256,32]{1,2,0:T(8,128)S(1)} all-to-all(f32[4,256,32]{1,2,0:T(8,128)S(1)} %copy.32), channel_id=1, replica_groups=mesh['rows'=8,'cols'=4] {'cols'}, dimensions={0} | all-to-all | bytes 262144 | tf_op jit(solution)/shard_map/all_to_all | solution.py:219
  208.9 0.1 copy.33
  209.0 0.7 reshape.14
  (28 shorter events, 0.4 us)
Async XLA Ops:
  6.5 31.0 %all-gather.3.cloned.1.call-start = ((), (), s32[]{:S(2)}) async-start(), calls=%async_computation.3 | async-start | bytes 1769472 | tf_op jit(solution)/shard_map/all_gather | solution.py:195
  8.2 112.8 %all-gather.5.cloned.1.call-start = ((), (), s32[]{:S(2)}) async-start(), calls=%async_computation.4 | async-start | bytes 5242880 | tf_op jit(solution)/shard_map/all_gather | solution.py:198
  37.5 1.2 slice-start
  38.8 2.1 copy-start.5
  38.8 2.2 %copy-start.4 = (s32[512]{0:T(512)S(1)}, s32[512]{0:T(512)}, u32[]{:S(2)}) copy-start(s32[512]{0:T(512)} %param.9) | copy-start | bytes 6148
  38.8 2.4 %copy-start.6 = (s32[512]{0:T(512)S(1)}, s32[512]{0:T(512)}, u32[]{:S(2)}) copy-start(s32[512]{0:T(512)} %param.10) | copy-start | bytes 6148
  38.8 2.4 %copy-start = (s32[512,128]{1,0:T(8,128)S(1)}, s32[512,128]{1,0:T(8,128)}, u32[]{:S(2)}) copy-start(s32[512,128]{1,0:T(8,128)} %third_ref.1) | copy-start | bytes 786436
  38.8 2.4 %copy-start.1 = (bf16[512,128]{1,0:T(8,128)(2,1)S(1)}, bf16[512,128]{1,0:T(8,128)(2,1)}, u32[]{:S(2)}) copy-start(bf16[512,128]{1,0:T(8,128)(2,1)} %values_ref.1) | copy-start | bytes 393220
  40.1 120.4 %all-reduce.2.cloned.1.call-start = ((), (), s32[]{:S(2)}) async-start(), calls=%async_computation.6 | async-start | bytes 1048576 | tf_op jit(solution)/shard_map/psum | solution.py:205
  41.2 38.7 %slice-start.1 = ((bf16[3072,256]{0,1:T(8,128)(2,1)}), bf16[1024,256]{0,1:T(8,128)(2,1)S(1)}, s32[]{:S(2)}) async-start(bf16[3072,256]{0,1:T(8,128)(2,1)} %all-gather.3.cloned.1.call-done), calls=%async_computation.8 | async-start | bytes 1048576
  76.7 3.2 %copy-start.2 = (bf16[32,512,256]{2,1,0:T(8,128)(2,1)}, bf16[32,512,256]{2,1,0:T(8,128)(2,1)S(1)}, u32[]{:S(2)}) copy-start(bf16[32,512,256]{2,1,0:T(8,128)(2,1)S(1)} %get-tuple-element.7.high_ref) | copy-start | bytes 25165828
  79.9 1.4 copy-start.3
  83.0 105.8 %reduce-scatter.2.cloned.1.call-start = ((), (), s32[]{:S(2)}) async-start(), calls=%async_computation.5 | async-start | bytes 655360 | tf_op jit(solution)/shard_map/reduce_scatter | solution.py:217
Sparse Core Ops, SparseCore 0:
  9.2 28.2 all-gather.2
  40.2 80.7 all-gather.4
  123.4 37.1 all-reduce.1
  162.7 21.6 reduce-scatter.1
